TPU v7x, 256 devices: a whole 4x4x8 slice. The times are simulated.
256 devices in a mesh: set: 32 (over y, x, core), path: 8 (over z).
Axes of the slice: x: 4, y: 4, z: 8, core: 2. Of those that a mesh axis runs over, the one named last changes fastest.
Arguments:
- start_state: float32 [4096, 2048], P(('path', 'set')), may hold values from -6 to 6
- shocks: bfloat16 [2, 4096, 2048], P(None, ('path', 'set')), may hold values from -6 to 6
- loading: bfloat16 [2048, 2048], replicated, may hold values from -0.125 to 0.125
- decay: float32 [2048], replicated, may hold values from 0.5 to 1
- factor_lists: int32 [4096, 64], P('set'), may hold values from 0 to 2047, all different within a row
- delta: bfloat16 [4096, 64], P('set'), may hold values from -0.75 to 0.75
- gamma: bfloat16 [4096, 64, 64], P('set'), may hold values from -0.09375 to 0.09375
- currency: int32 [4096], P('set'), may hold values from 0 to 15
- owner: int32 [4096], P('set'), may hold values from 0 to 255
Outputs:
- exposure: float32 [2, 256, 4096], P(None, 'set', 'path')
- end_state: float32 [4096, 2048], P(('path', 'set'))
Inputs may be any that keep to these rules, and one draw needn't show every extreme that they name: `factor_lists`: the 64 factors of one netting set are different.
All inputs are finite; a program needn't handle non-finite values.
Results may differ from a plain program's by a relative error of at most 0.004.
Values may be sent and summed in bfloat16 or wider, within the bound.
No kernel may reach another device: no remote copies, remote signals or barrier semaphores. Data moves between devices by JAX's collectives and lax.ppermute only.
A program may use at most 64 MiB of HBM per device.

v0:
```python
import math
import jax
import jax.numpy as jnp
from jax import lax
from jax.sharding import PartitionSpec as P

NB = 16
STEPS = 2
PDEV = 16
CP_DEV = 8


def value_block(slab, lists_b, delta_b, gamma_b, cur_b):
    rows = slab.shape[0]
    count = lists_b.shape[0]
    picked = jnp.take(slab, lists_b.reshape(-1), axis=1).reshape(rows, count, lists_b.shape[1])
    curved = jnp.einsum("psk,skl->psl", picked, gamma_b, preferred_element_type=jnp.float32)
    linear = delta_b.astype(jnp.float32)[None] + 0.5 * curved
    local = jnp.sum(picked.astype(jnp.float32) * linear, axis=2)
    rates = jnp.exp(0.2 * jnp.take(slab, cur_b, axis=1).astype(jnp.float32))
    return (local * rates).T


def revalue(slab, lists, delta, gamma, cur):
    total = lists.shape[0]
    width = math.gcd(16, total)
    blocks = total // width
    depth = lists.shape[1]
    stacked = lax.map(
        lambda a: value_block(slab, a[0], a[1], a[2], a[3]),
        (
            lists.reshape(blocks, width, depth),
            delta.reshape(blocks, width, depth),
            gamma.reshape(blocks, width, depth, depth),
            cur.reshape(blocks, width),
        ),
    )
    return stacked.reshape(total, slab.shape[0])


def regress(gram, moments, total):
    size = gram.shape[0]
    chol = jnp.linalg.cholesky(gram / total + 0.001 * jnp.eye(size, dtype=jnp.float32))
    middle = lax.linalg.triangular_solve(chol, moments / total, left_side=True, lower=True)
    return lax.linalg.triangular_solve(chol, middle, left_side=True, lower=True, transpose_a=True)


def per_device(start_state, shocks, loading, decay, factor_lists, delta, gamma, currency, owner):
    high = lax.Precision.HIGHEST
    groups = lax.axis_size("set")
    member = lax.axis_index("set")
    total_paths = PDEV * groups * lax.axis_size("path")
    set_count = factor_lists.shape[0]
    onehot = (owner[None, :] == jnp.arange(CP_DEV * groups, dtype=jnp.int32)[:, None]).astype(
        jnp.float32
    )
    state = start_state
    slabs = []
    evaluated = []
    for step in range(STEPS):
        state = decay[None, :] * state + jnp.dot(
            shocks[step], loading, preferred_element_type=jnp.float32
        )
        slab = state.astype(jnp.bfloat16)
        slabs.append(slab)
        piece = lax.all_gather(slab, "set", axis=0, tiled=True)
        evaluate_values = revalue(piece, factor_lists, delta, gamma, currency)
        evaluated.append(
            jnp.concatenate([evaluate_values, piece[:, :NB].astype(jnp.float32).T], axis=0)
        )
    results = []
    for step in range(STEPS):
        values = evaluated[step][:set_count]
        factors = evaluated[step][set_count:]
        summed = lax.psum(jnp.dot(onehot, values, precision=high), "set")
        netted = lax.dynamic_slice_in_dim(summed, member * CP_DEV, CP_DEV, 0)
        ones = jnp.ones((1, values.shape[1]), jnp.float32)
        basis = jnp.concatenate([ones, factors], axis=0)
        gram, moments = lax.psum(
            (jnp.dot(basis, basis.T, precision=high), jnp.dot(basis, netted.T, precision=high)),
            "path",
        )
        coef = regress(gram, moments, total_paths)
        fitted = jnp.dot(coef.T, basis, precision=high)
        results.append(jnp.maximum(netted - 0.9 * fitted, 0.0))
    return (jnp.stack(results), state)


def solution(mesh):
    return jax.shard_map(
        per_device,
        mesh=mesh,
        in_specs=(
            P(("path", "set"), None),
            P(None, ("path", "set"), None),
            P(),
            P(),
            P("set", None),
            P("set", None),
            P("set", None, None),
            P("set"),
            P("set"),
        ),
        out_specs=(P(None, "set", "path"), P(("path", "set"), None)),
        check_vma=False,
    )
```

profile of v0, /device:TPU:6, one launch (start us, length us, event | category | flops | bytes accessed | tf_op | source)
XLA Modules:
  0.0 349.1 jit_solution(17713936069963146569)
XLA Ops:
  7.2 5.4 %fusion.65 = (bf16[16,2048]{1,0:T(8,128)(2,1)}, f32[16,2048]{1,0:T(8,128)S(1)}) fusion(bf16[2048,2048]{1,0:T(8,128)(2,1)} %param.24, bf16[2,16,2048]{2,1,0:T(8,128)(2,1)} %param.23, f32[16,2048]{1,0:T(8,128)} %param.22, f32[2048]{0:T(1024)} %param.25), kind=kOutput, calls=%fused_computation.112 | convolution fusion | flops 134316032 | bytes 8790016 | tf_op jit(solution)/shard_map/dot_general | solution.py:61
  13.1 1.9 fusion.64
  15.1 0.7 all-gather.3.cloned.1.call-update
  16.2 4.5 %copy.13 = bf16[128,64,64]{1,2,0:T(8,128)(2,1)} copy(bf16[128,64,64]{0,2,1:T(8,128)(2,1)S(1)} %copy-done.1) | data formatting | bytes 2097152 | tf_op args[6]
  20.7 45.6 %all-gather.5.cloned.1.call-done = bf16[512,2048]{1,0:T(8,128)(2,1)} async-done(((bf16[16,2048]{1,0:T(8,128)(2,1)}), bf16[512,2048]{1,0:T(8,128)(2,1)}) %all-gather.5.cloned.1.call-update) | async-done | bytes 2097168 | tf_op jit(solution)/shard_map/all_gather | solution.py:66
  66.3 2.9 copy.17
  69.2 52.6 %while.21 = (s32[]{:T(128)}, f32[8,16,512]{2,1,0:T(8,128)S(1)}, s32[8,16,64]{2,1,0:T(8,128)S(1)}, bf16[512,2048]{0,1:T(8,128)(2,1)S(1)}, bf16[8,16,64]{2,1,0:T(8...) while((s32[]{:T(128)}, f32[8,16,512]{2,1,0:T(8,128)S(1)}, ...), condition=%wide.region_10.16_spmd, body=%wide.region_8.15_spmd.sunk | while | flops 70291552 | bytes 6755201 | solution.py:29
  69.4 0.6 gather_fusion.3
  70.0 4.0 %gather_fusion.2 = bf16[1024,512]{1,0:T(8,128)(2,1)S(1)} fusion(bf16[512,2048]{0,1:T(8,128)(2,1)S(1)} %get-tuple-element.254, s32[1024]{0:T(1024)S(1)} %fusion.90), kind=kCustom, calls=%fused_computation.2.clone.clone.1 | custom fusion | bytes 2101248 | tf_op jit(solution)/shard_map/while/body/eval_jaxpr/jit(_take)/gather | solution.py:16
  74.2 1.5 fusion.91
  76.0 0.6 gather_fusion.3
  76.6 4.0 %gather_fusion.2 = bf16[1024,512]{1,0:T(8,128)(2,1)S(1)} fusion(bf16[512,2048]{0,1:T(8,128)(2,1)S(1)} %get-tuple-element.254, s32[1024]{0:T(1024)S(1)} %fusion.90), kind=kCustom, calls=%fused_computation.2.clone.clone.1 | custom fusion | bytes 2101248 | tf_op jit(solution)/shard_map/while/body/eval_jaxpr/jit(_take)/gather | solution.py:16
  80.7 1.5 fusion.91
  82.5 0.6 gather_fusion.3
  83.1 4.0 %gather_fusion.2 = bf16[1024,512]{1,0:T(8,128)(2,1)S(1)} fusion(bf16[512,2048]{0,1:T(8,128)(2,1)S(1)} %get-tuple-element.254, s32[1024]{0:T(1024)S(1)} %fusion.90), kind=kCustom, calls=%fused_computation.2.clone.clone.1 | custom fusion | bytes 2101248 | tf_op jit(solution)/shard_map/while/body/eval_jaxpr/jit(_take)/gather | solution.py:16
  87.3 1.5 fusion.91
  89.7 4.0 %gather_fusion.2 = bf16[1024,512]{1,0:T(8,128)(2,1)S(1)} fusion(bf16[512,2048]{0,1:T(8,128)(2,1)S(1)} %get-tuple-element.254, s32[1024]{0:T(1024)S(1)} %fusion.90), kind=kCustom, calls=%fused_computation.2.clone.clone.1 | custom fusion | bytes 2101248 | tf_op jit(solution)/shard_map/while/body/eval_jaxpr/jit(_take)/gather | solution.py:16
  93.9 1.5 fusion.91
  96.3 4.0 %gather_fusion.2 = bf16[1024,512]{1,0:T(8,128)(2,1)S(1)} fusion(bf16[512,2048]{0,1:T(8,128)(2,1)S(1)} %get-tuple-element.254, s32[1024]{0:T(1024)S(1)} %fusion.90), kind=kCustom, calls=%fused_computation.2.clone.clone.1 | custom fusion | bytes 2101248 | tf_op jit(solution)/shard_map/while/body/eval_jaxpr/jit(_take)/gather | solution.py:16
  100.5 1.5 fusion.91
  102.8 4.0 %gather_fusion.2 = bf16[1024,512]{1,0:T(8,128)(2,1)S(1)} fusion(bf16[512,2048]{0,1:T(8,128)(2,1)S(1)} %get-tuple-element.254, s32[1024]{0:T(1024)S(1)} %fusion.90), kind=kCustom, calls=%fused_computation.2.clone.clone.1 | custom fusion | bytes 2101248 | tf_op jit(solution)/shard_map/while/body/eval_jaxpr/jit(_take)/gather | solution.py:16
  107.0 1.5 fusion.91
  109.4 4.0 %gather_fusion.2 = bf16[1024,512]{1,0:T(8,128)(2,1)S(1)} fusion(bf16[512,2048]{0,1:T(8,128)(2,1)S(1)} %get-tuple-element.254, s32[1024]{0:T(1024)S(1)} %fusion.90), kind=kCustom, calls=%fused_computation.2.clone.clone.1 | custom fusion | bytes 2101248 | tf_op jit(solution)/shard_map/while/body/eval_jaxpr/jit(_take)/gather | solution.py:16
  113.6 1.5 fusion.91
  116.0 4.0 %gather_fusion.2 = bf16[1024,512]{1,0:T(8,128)(2,1)S(1)} fusion(bf16[512,2048]{0,1:T(8,128)(2,1)S(1)} %get-tuple-element.254, s32[1024]{0:T(1024)S(1)} %fusion.90), kind=kCustom, calls=%fused_computation.2.clone.clone.1 | custom fusion | bytes 2101248 | tf_op jit(solution)/shard_map/while/body/eval_jaxpr/jit(_take)/gather | solution.py:16
  120.2 1.5 fusion.91
  121.8 0.7 copy-done.2
  122.5 2.9 copy.14
  125.4 52.6 %while.20 = (s32[]{:T(128)}, f32[8,16,512]{2,1,0:T(8,128)S(1)}, s32[8,16,64]{2,1,0:T(8,128)S(1)}, bf16[512,2048]{0,1:T(8,128)(2,1)S(1)}, bf16[8,16,64]{2,1,0:T(8...) while((s32[]{:T(128)}, f32[8,16,512]{2,1,0:T(8,128)S(1)}, ...), condition=%wide.region_2.5_spmd, body=%wide.region_0.4_spmd.sunk | while | flops 70291552 | bytes 6755201 | solution.py:29
  126.2 4.0 %gather_fusion = bf16[1024,512]{1,0:T(8,128)(2,1)S(1)} fusion(bf16[512,2048]{0,1:T(8,128)(2,1)S(1)} %get-tuple-element.278, s32[1024]{0:T(1024)S(1)} %fusion.86), kind=kCustom, calls=%fused_computation.clone.clone.1 | custom fusion | bytes 2101248 | tf_op jit(solution)/shard_map/while/body/eval_jaxpr/jit(_take)/gather | solution.py:16
  130.4 1.5 fusion.87
  132.8 4.0 %gather_fusion = bf16[1024,512]{1,0:T(8,128)(2,1)S(1)} fusion(bf16[512,2048]{0,1:T(8,128)(2,1)S(1)} %get-tuple-element.278, s32[1024]{0:T(1024)S(1)} %fusion.86), kind=kCustom, calls=%fused_computation.clone.clone.1 | custom fusion | bytes 2101248 | tf_op jit(solution)/shard_map/while/body/eval_jaxpr/jit(_take)/gather | solution.py:16
  136.9 1.5 fusion.87
  139.3 4.0 %gather_fusion = bf16[1024,512]{1,0:T(8,128)(2,1)S(1)} fusion(bf16[512,2048]{0,1:T(8,128)(2,1)S(1)} %get-tuple-element.278, s32[1024]{0:T(1024)S(1)} %fusion.86), kind=kCustom, calls=%fused_computation.clone.clone.1 | custom fusion | bytes 2101248 | tf_op jit(solution)/shard_map/while/body/eval_jaxpr/jit(_take)/gather | solution.py:16
  143.5 1.5 fusion.87
  145.9 4.0 %gather_fusion = bf16[1024,512]{1,0:T(8,128)(2,1)S(1)} fusion(bf16[512,2048]{0,1:T(8,128)(2,1)S(1)} %get-tuple-element.278, s32[1024]{0:T(1024)S(1)} %fusion.86), kind=kCustom, calls=%fused_computation.clone.clone.1 | custom fusion | bytes 2101248 | tf_op jit(solution)/shard_map/while/body/eval_jaxpr/jit(_take)/gather | solution.py:16
  150.1 1.5 fusion.87
  152.5 4.0 %gather_fusion = bf16[1024,512]{1,0:T(8,128)(2,1)S(1)} fusion(bf16[512,2048]{0,1:T(8,128)(2,1)S(1)} %get-tuple-element.278, s32[1024]{0:T(1024)S(1)} %fusion.86), kind=kCustom, calls=%fused_computation.clone.clone.1 | custom fusion | bytes 2101248 | tf_op jit(solution)/shard_map/while/body/eval_jaxpr/jit(_take)/gather | solution.py:16
  156.7 1.5 fusion.87
  159.0 4.0 %gather_fusion = bf16[1024,512]{1,0:T(8,128)(2,1)S(1)} fusion(bf16[512,2048]{0,1:T(8,128)(2,1)S(1)} %get-tuple-element.278, s32[1024]{0:T(1024)S(1)} %fusion.86), kind=kCustom, calls=%fused_computation.clone.clone.1 | custom fusion | bytes 2101248 | tf_op jit(solution)/shard_map/while/body/eval_jaxpr/jit(_take)/gather | solution.py:16
  163.2 1.5 fusion.87
  165.6 4.0 %gather_fusion = bf16[1024,512]{1,0:T(8,128)(2,1)S(1)} fusion(bf16[512,2048]{0,1:T(8,128)(2,1)S(1)} %get-tuple-element.278, s32[1024]{0:T(1024)S(1)} %fusion.86), kind=kCustom, calls=%fused_computation.clone.clone.1 | custom fusion | bytes 2101248 | tf_op jit(solution)/shard_map/while/body/eval_jaxpr/jit(_take)/gather | solution.py:16
  169.8 1.5 fusion.87
  172.2 4.0 %gather_fusion = bf16[1024,512]{1,0:T(8,128)(2,1)S(1)} fusion(bf16[512,2048]{0,1:T(8,128)(2,1)S(1)} %get-tuple-element.278, s32[1024]{0:T(1024)S(1)} %fusion.86), kind=kCustom, calls=%fused_computation.clone.clone.1 | custom fusion | bytes 2101248 | tf_op jit(solution)/shard_map/while/body/eval_jaxpr/jit(_take)/gather | solution.py:16
  176.4 1.5 fusion.87
  178.0 1.2 fusion.19
  179.2 2.2 fusion.18
  181.4 0.9 slice_bitcast_fusion.1
  182.6 0.9 slice_bitcast_fusion
  183.9 113.8 %all-reduce.6.cloned.1.call-done = (f32[256,512]{1,0:T(8,128)}, f32[256,512]{1,0:T(8,128)}) async-done(((f32[256,512]{1,0:T(8,128)}, f32[256,512]{1,0:T(8,128)}), (f32[256,512]{1,0:T(8,128)}, f32[256,512]{1,0:T(8,128)})) %all-reduce.6.cloned.1.call-update) | async-done | bytes 1048592 | tf_op jit(solution)/shard_map/psum | solution.py:75
  297.7 1.1 fusion.20
  298.7 1.1 fusion.25
  299.8 30.7 %all-reduce.3 = (f32[17,17]{0,1:T(8,128)S(1)}, f32[17,8]{1,0:T(8,128)S(1)}, f32[17,17]{0,1:T(8,128)S(1)}, f32[17,8]{1,0:T(8,128)S(1)}) all-reduce(f32[17,17]{0,1:T(8,128)S(1)} %fusion.22, f32[17,8]{1,0:T(8,128)S(1)} %fusion.20, f32[17,17]{0,1:T(8,128)S(1)} %fusion.27, ...), channel_id=1, replica_groups=mesh['set'=32,'path'=8] {'path'}, use_global_device_ids=true, to_apply=%region_12.18 | all-reduce | flops 850 | bytes 6800 | tf_op jit(solution)/shard_map/psum | solution.py:79
  330.6 1.5 cholesky.55
  332.2 0.6 compare_reduce_fusion
  332.9 0.6 fusion.39
  333.5 1.3 custom-call.13
  335.2 1.1 fusion.14
  336.4 1.5 cholesky.44
  337.9 0.6 compare_reduce_fusion.1
  338.6 0.6 fusion.38
  339.2 1.3 custom-call.11
  340.9 1.1 fusion.17
  342.0 0.6 pad_maximum_fusion
  (198 shorter events, 17.0 us)
Async XLA Ops:
  7.2 5.4 %copy-start.4 = (f32[2048]{0:T(1024)S(1)}, f32[2048]{0:T(1024)}, u32[]{:S(2)}) copy-start(f32[2048]{0:T(1024)} %param.25) | copy-start | bytes 24580
  7.2 5.4 %copy-start.3 = (bf16[2,16,2048]{2,1,0:T(8,128)(2,1)S(1)}, bf16[2,16,2048]{2,1,0:T(8,128)(2,1)}, u32[]{:S(2)}) copy-start(bf16[2,16,2048]{2,1,0:T(8,128)(2,1)} %param.23) | copy-start | bytes 393220
  7.2 59.2 %all-gather.5.cloned.1.call-start = ((), (), s32[]{:S(2)}) async-start(), calls=%async_computation.1 | async-start | bytes 2162688 | tf_op jit(solution)/shard_map/all_gather | solution.py:66
  7.2 5.9 %copy-start = (bf16[2048,2048]{1,0:T(8,128)(2,1)S(1)}, bf16[2048,2048]{1,0:T(8,128)(2,1)}, u32[]{:S(2)}) copy-start(bf16[2048,2048]{1,0:T(8,128)(2,1)} %param.24) | copy-start | bytes 25165828
  13.1 2.7 copy-start.8
  13.1 2.8 copy-start.6
  13.1 2.9 copy-start.5
  13.1 3.0 copy-start.1
  15.0 106.8 %all-gather.3.cloned.1.call-start = ((), (), s32[]{:S(2)}) async-start(), calls=%async_computation | async-start | bytes 2162688 | tf_op jit(solution)/shard_map/all_gather | solution.py:66
  15.8 281.9 %all-reduce.6.cloned.1.call-start = ((), (), s32[]{:S(2)}) async-start(), calls=%async_computation.2 | async-start | bytes 2097152 | tf_op jit(solution)/shard_map/psum | solution.py:75
  121.8 0.7 copy-start.2
  125.4 52.6 %copy-start.7 = (s32[128]{0:T(128)S(1)}, s32[128]{0:T(128)}, u32[]{:S(2)}) copy-start(s32[128]{0:T(128)} %param.30) | copy-start | bytes 1540
Sparse Core Ops, SparseCore 0:
  15.2 51.1 all-gather.4
  68.9 47.9 all-gather.2
  181.5 116.0 all-reduce.5
where the time goes:
time: 350 us; the launch traced here: 349 us
  waiting for transfers between devices  160 us (46%)
  local copies, waits for them, and re-layouts  87.9 us (25%)
  matrix products  40.6 us (12%)
  blocking collectives  30.7 us (9%)
  other arithmetic  14.4 us (4%)
  between operations  14 us (4%)
    psum x1, waiting for transfers between devices, per_device(): summed = lax.psum(jnp.dot(onehot, values, precision=high), 'set')  114 us
    gather x16, local copies, waits for them, and re-layouts, value_block(): jnp.take(slab, lists_b.reshape(-1), axis=1)  63.4 us
    all_gather x2, waiting for transfers between devices, per_device(): piece = lax.all_gather(slab, 'set', axis=0, tiled=True)  45.7 us
    psum x1, blocking collectives, per_device(): lax.psum((jnp.dot(basis, basis.T, precision=high), jnp.dot(basis, netted....  30.7 us
    dot_general x16, matrix products, value_block(): jnp.einsum('psk,skl->psl', picked, gamma_b, preferred_element_type=jnp.fl...  24.4 us
    gather x16, local copies, waits for them, and re-layouts, value_block(): rates = jnp.exp(0.2 * jnp.take(slab, cur_b, axis=1).astype(jnp.float32))  9.44 us
    dot_general x2, matrix products, per_device(): jnp.dot(shocks[step], loading, preferred_element_type=jnp.float32)  7.25 us
  transfers between devices with their start and end apart: 3, of which 2 were waited for; matrix products, arithmetic and copies ran while one was open for 18% of the time, Pallas kernels for 0%

commit v1 on v0

--- a/solution.py
+++ b/solution.py
@@ -63,7 +63,15 @@
         )
         slab = state.astype(jnp.bfloat16)
         slabs.append(slab)
-        piece = lax.all_gather(slab, "set", axis=0, tiled=True)
+        piece = jnp.concatenate(
+            lax.all_to_all(
+                jnp.stack([slab for _ in range(lax.axis_size("set"))]),
+                axis_name="set",
+                split_axis=0,
+                concat_axis=0,
+            ),
+            axis=0,
+        )
         evaluate_values = revalue(piece, factor_lists, delta, gamma, currency)
         evaluated.append(
             jnp.concatenate([evaluate_values, piece[:, :NB].astype(jnp.float32).T], axis=0)

time: 350 us -> 403 us (1.15)
  blocking collectives: 30.7 us -> 63.9 us
  local copies, waits for them, and re-layouts: 87.9 us -> 120 us
  waiting for transfers between devices: 160 us -> 135 us
  starting transfers between devices: 0.12 us -> 7.41 us
  other arithmetic: 14.4 us -> 19.3 us
    all_gather x2 -> x0, waiting for transfers between devices: 45.7 us -> none  [per_device(): piece = lax.all_gather(slab, 'set', axis=0, tiled=True)]
    all_to_all x0 -> x1, blocking collectives: none -> 33.2 us  [per_device(): lax.all_to_all(jnp.stack([slab for _ in range(lax.axis_size('set'))]), ax...]
    all_to_all x0 -> x1, waiting for transfers between devices: none -> 18 us  [per_device(): lax.all_to_all(jnp.stack([slab for _ in range(lax.axis_size('set'))]), ax...]
    gather x16, local copies, waits for them, and re-layouts: 63.4 us -> 78.5 us  [value_block(): jnp.take(slab, lists_b.reshape(-1), axis=1)]
    gather x16, local copies, waits for them, and re-layouts: 9.44 us -> 24.3 us  [value_block(): rates = jnp.exp(0.2 * jnp.take(slab, cur_b, axis=1).astype(jnp.float32))]
    all_to_all x0 -> x1, starting transfers between devices: none -> 7.37 us  [per_device(): lax.all_to_all(jnp.stack([slab for _ in range(lax.axis_size('set'))]), ax...]
    dynamic_update_slice x16, other arithmetic: 1.4 us -> 6.32 us  [revalue(): lax.map(lambda a: value_block(slab, a[0], a[1], a[2], a[3]), (lists.resha...]
  transfers between devices with their start and end apart: 3 -> 2, of which waited for: 2 -> 2; matrix products, arithmetic and copies ran while one was open for 18% -> 2% of each run, Pallas kernels for 0% -> 0%
where the time goes in v1:
time: 403 us; the launch traced here: 401 us
  waiting for transfers between devices  135 us (33%)
  local copies, waits for them, and re-layouts  120 us (30%)
  blocking collectives  63.9 us (16%)
  matrix products  39.9 us (10%)
  other arithmetic  19.3 us (5%)
  between operations  14.2 us (4%)
  starting transfers between devices  7.41 us (2%)
    psum x1, waiting for transfers between devices, per_device(): summed = lax.psum(jnp.dot(onehot, values, precision=high), 'set')  117 us
    gather x16, local copies, waits for them, and re-layouts, value_block(): jnp.take(slab, lists_b.reshape(-1), axis=1)  78.5 us
    all_to_all x1, blocking collectives, per_device(): lax.all_to_all(jnp.stack([slab for _ in range(lax.axis_size('set'))]), ax...  33.2 us
    psum x1, blocking collectives, per_device(): lax.psum((jnp.dot(basis, basis.T, precision=high), jnp.dot(basis, netted....  30.7 us
    dot_general x16, matrix products, value_block(): jnp.einsum('psk,skl->psl', picked, gamma_b, preferred_element_type=jnp.fl...  24.4 us
    gather x16, local copies, waits for them, and re-layouts, value_block(): rates = jnp.exp(0.2 * jnp.take(slab, cur_b, axis=1).astype(jnp.float32))  24.3 us
    all_to_all x1, waiting for transfers between devices, per_device(): lax.all_to_all(jnp.stack([slab for _ in range(lax.axis_size('set'))]), ax...  18 us
  transfers between devices with their start and end apart: 2, of which 2 were waited for; matrix products, arithmetic and copies ran while one was open for 2% of the time, Pallas kernels for 0%

profile of v1, /device:TPU:6, one launch (start us, length us, event | category | flops | bytes accessed | tf_op | source)
XLA Modules:
  0.0 401.3 jit_solution(3159381261575804764)
XLA Ops:
  7.2 4.7 %fusion.65 = (bf16[16,2048]{1,0:T(8,128)(2,1)S(1)}, f32[16,2048]{1,0:T(8,128)S(1)}) fusion(bf16[2048,2048]{1,0:T(8,128)(2,1)} %param.24, bf16[2,16,2048]{2,1,0:T(8,128)(2,1)} %param.23, f32[16,2048]{1,0:T(8,128)} %param.22, f32[2048]{0:T(1024)} %param.25), kind=kOutput, calls=%fused_computation.112 | convolution fusion | flops 134316032 | bytes 8790016 | tf_op jit(solution)/shard_map/dot_general | solution.py:61
  11.9 1.1 copy-done
  13.0 1.9 fusion.64
  15.1 33.2 %all_to_all.10 = bf16[32,16,2048]{2,1,0:T(8,128)(2,1)S(1)} all-to-all(bf16[32,16,2048]{2,1,0:T(8,128)(2,1)S(1)} %stack.12), channel_id=1, replica_groups=mesh['set'=32,'path'=8] {'set'}, dimensions={0} | all-to-all | bytes 4194304 | tf_op jit(solution)/shard_map/all_to_all | solution.py:67
  48.3 1.8 stack.10
  50.2 7.4 %all-to-all-start = ((bf16[32,16,2048]{2,1,0:T(8,128)(2,1)}), bf16[32,16,2048]{2,1,0:T(8,128)(2,1)}, u32[]{:S(2)}, u32[]{:S(2)}) async-start(bf16[32,16,2048]{2,1,0:T(8,128)(2,1)} %stack.10), calls=%async_computation | async-start | bytes 4194304 | tf_op jit(solution)/shard_map/all_to_all | solution.py:67
  57.9 4.5 %copy.22 = bf16[128,64,64]{1,2,0:T(8,128)(2,1)} copy(bf16[128,64,64]{0,2,1:T(8,128)(2,1)S(1)} %copy-done.2) | data formatting | bytes 2097152 | tf_op args[6]
  62.4 2.5 copy.26
  65.0 18.0 %all-to-all-done = bf16[32,16,2048]{2,1,0:T(8,128)(2,1)} async-done(((bf16[32,16,2048]{2,1,0:T(8,128)(2,1)}), bf16[32,16,2048]{2,1,0:T(8,128)(2,1)}, u32[]{:S(2)}, u32[]{:S(2)}) %all-to-all-start) | async-done | bytes 2097184 | tf_op jit(solution)/shard_map/all_to_all | solution.py:67
  82.9 2.9 copy.23
  86.6 87.3 %while.21 = (s32[]{:T(128)}, f32[8,16,512]{2,1,0:T(8,128)}, s32[8,16,64]{2,1,0:T(8,128)S(1)}, bf16[512,2048]{0,1:T(8,128)(2,1)}, bf16[8,16,64]{2,1,0:T(8,128)(2,...) while((s32[]{:T(128)}, f32[8,16,512]{2,1,0:T(8,128)}, ...), condition=%wide.region_10.16_spmd, body=%wide.region_8.15_spmd.sunk | while | flops 70291552 | bytes 6754705 | solution.py:29
  86.7 2.5 gather_fusion.3
  89.2 5.9 %gather_fusion.2 = bf16[1024,512]{1,0:T(8,128)(2,1)S(1)} fusion(bf16[512,2048]{0,1:T(8,128)(2,1)} %get-tuple-element.254, s32[1024]{0:T(1024)S(1)} %fusion.90), kind=kCustom, calls=%fused_computation.2.clone.clone.1 | custom fusion | bytes 2101248 | tf_op jit(solution)/shard_map/while/body/eval_jaxpr/jit(_take)/gather | solution.py:16
  95.3 1.5 fusion.91
  97.6 2.5 gather_fusion.3
  100.1 5.9 %gather_fusion.2 = bf16[1024,512]{1,0:T(8,128)(2,1)S(1)} fusion(bf16[512,2048]{0,1:T(8,128)(2,1)} %get-tuple-element.254, s32[1024]{0:T(1024)S(1)} %fusion.90), kind=kCustom, calls=%fused_computation.2.clone.clone.1 | custom fusion | bytes 2101248 | tf_op jit(solution)/shard_map/while/body/eval_jaxpr/jit(_take)/gather | solution.py:16
  106.2 1.5 fusion.91
  108.5 2.5 gather_fusion.3
  111.0 5.9 %gather_fusion.2 = bf16[1024,512]{1,0:T(8,128)(2,1)S(1)} fusion(bf16[512,2048]{0,1:T(8,128)(2,1)} %get-tuple-element.254, s32[1024]{0:T(1024)S(1)} %fusion.90), kind=kCustom, calls=%fused_computation.2.clone.clone.1 | custom fusion | bytes 2101248 | tf_op jit(solution)/shard_map/while/body/eval_jaxpr/jit(_take)/gather | solution.py:16
  117.1 1.5 fusion.91
  119.5 2.5 gather_fusion.3
  121.9 5.9 %gather_fusion.2 = bf16[1024,512]{1,0:T(8,128)(2,1)S(1)} fusion(bf16[512,2048]{0,1:T(8,128)(2,1)} %get-tuple-element.254, s32[1024]{0:T(1024)S(1)} %fusion.90), kind=kCustom, calls=%fused_computation.2.clone.clone.1 | custom fusion | bytes 2101248 | tf_op jit(solution)/shard_map/while/body/eval_jaxpr/jit(_take)/gather | solution.py:16
  128.0 1.5 fusion.91
  130.4 2.5 gather_fusion.3
  132.8 5.9 %gather_fusion.2 = bf16[1024,512]{1,0:T(8,128)(2,1)S(1)} fusion(bf16[512,2048]{0,1:T(8,128)(2,1)} %get-tuple-element.254, s32[1024]{0:T(1024)S(1)} %fusion.90), kind=kCustom, calls=%fused_computation.2.clone.clone.1 | custom fusion | bytes 2101248 | tf_op jit(solution)/shard_map/while/body/eval_jaxpr/jit(_take)/gather | solution.py:16
  138.9 1.5 fusion.91
  141.3 2.5 gather_fusion.3
  143.7 5.9 %gather_fusion.2 = bf16[1024,512]{1,0:T(8,128)(2,1)S(1)} fusion(bf16[512,2048]{0,1:T(8,128)(2,1)} %get-tuple-element.254, s32[1024]{0:T(1024)S(1)} %fusion.90), kind=kCustom, calls=%fused_computation.2.clone.clone.1 | custom fusion | bytes 2101248 | tf_op jit(solution)/shard_map/while/body/eval_jaxpr/jit(_take)/gather | solution.py:16
  149.8 1.5 fusion.91
  152.2 2.5 gather_fusion.3
  154.6 5.9 %gather_fusion.2 = bf16[1024,512]{1,0:T(8,128)(2,1)S(1)} fusion(bf16[512,2048]{0,1:T(8,128)(2,1)} %get-tuple-element.254, s32[1024]{0:T(1024)S(1)} %fusion.90), kind=kCustom, calls=%fused_computation.2.clone.clone.1 | custom fusion | bytes 2101248 | tf_op jit(solution)/shard_map/while/body/eval_jaxpr/jit(_take)/gather | solution.py:16
  160.7 1.5 fusion.91
  163.1 2.5 gather_fusion.3
  165.5 5.9 %gather_fusion.2 = bf16[1024,512]{1,0:T(8,128)(2,1)S(1)} fusion(bf16[512,2048]{0,1:T(8,128)(2,1)} %get-tuple-element.254, s32[1024]{0:T(1024)S(1)} %fusion.90), kind=kCustom, calls=%fused_computation.2.clone.clone.1 | custom fusion | bytes 2101248 | tf_op jit(solution)/shard_map/while/body/eval_jaxpr/jit(_take)/gather | solution.py:16
  171.6 1.5 fusion.91
  173.9 52.6 %while.20 = (s32[]{:T(128)}, f32[8,16,512]{2,1,0:T(8,128)S(1)}, s32[8,16,64]{2,1,0:T(8,128)S(1)}, bf16[512,2048]{0,1:T(8,128)(2,1)S(1)}, bf16[8,16,64]{2,1,0:T(8...) while((s32[]{:T(128)}, f32[8,16,512]{2,1,0:T(8,128)S(1)}, ...), condition=%wide.region_2.5_spmd, body=%wide.region_0.4_spmd.sunk | while | flops 70291552 | bytes 6755201 | solution.py:29
  174.7 4.0 gather_fusion
  178.8 1.5 fusion.87
  181.2 4.0 gather_fusion
  185.4 1.5 fusion.87
  187.8 4.0 gather_fusion
  192.0 1.5 fusion.87
  194.4 4.0 gather_fusion
  198.6 1.5 fusion.87
  200.9 4.0 gather_fusion
  205.1 1.5 fusion.87
  207.5 4.0 gather_fusion
  211.7 1.5 fusion.87
  214.1 4.0 gather_fusion
  218.3 1.5 fusion.87
  220.7 4.0 gather_fusion
  224.8 1.5 fusion.87
  226.5 1.2 fusion.19
  227.7 2.1 fusion.18
  232.3 117.2 %all-reduce.6.cloned.1.call-done = (f32[256,512]{1,0:T(8,128)}, f32[256,512]{1,0:T(8,128)}) async-done(((f32[256,512]{1,0:T(8,128)}, f32[256,512]{1,0:T(8,128)}), (f32[256,512]{1,0:T(8,128)}, f32[256,512]{1,0:T(8,128)})) %all-reduce.6.cloned.1.call-update) | async-done | bytes 1048592 | tf_op jit(solution)/shard_map/psum | solution.py:83
  349.5 1.1 fusion.20
  350.6 1.1 fusion.25
  351.7 30.7 %all-reduce.3 = (f32[17,17]{0,1:T(8,128)S(1)}, f32[17,8]{1,0:T(8,128)S(1)}, f32[17,17]{0,1:T(8,128)S(1)}, f32[17,8]{1,0:T(8,128)S(1)}) all-reduce(f32[17,17]{0,1:T(8,128)S(1)} %fusion.22, f32[17,8]{1,0:T(8,128)S(1)} %fusion.20, f32[17,17]{0,1:T(8,128)S(1)} %fusion.27, ...), channel_id=1, replica_groups=mesh['set'=32,'path'=8] {'path'}, use_global_device_ids=true, to_apply=%region_12.18 | all-reduce | flops 850 | bytes 6800 | tf_op jit(solution)/shard_map/psum | solution.py:87
  382.5 1.5 cholesky.55
  385.4 1.3 custom-call.13
  387.1 1.1 fusion.14
  388.2 1.5 cholesky.44
  391.1 1.3 custom-call.11
  392.8 1.1 fusion.17
  (197 shorter events, 24.4 us)
Async XLA Ops:
  7.2 4.8 %copy-start.4 = (f32[2048]{0:T(1024)S(1)}, f32[2048]{0:T(1024)}, u32[]{:S(2)}) copy-start(f32[2048]{0:T(1024)} %param.25) | copy-start | bytes 24580
  7.2 5.8 %copy-start = (bf16[2048,2048]{1,0:T(8,128)(2,1)S(1)}, bf16[2048,2048]{1,0:T(8,128)(2,1)}, u32[]{:S(2)}) copy-start(bf16[2048,2048]{1,0:T(8,128)(2,1)} %param.24) | copy-start | bytes 25165828
  7.2 5.8 %copy-start.3 = (bf16[2,16,2048]{2,1,0:T(8,128)(2,1)S(1)}, bf16[2,16,2048]{2,1,0:T(8,128)(2,1)}, u32[]{:S(2)}) copy-start(bf16[2,16,2048]{2,1,0:T(8,128)(2,1)} %param.23) | copy-start | bytes 393220
  48.3 14.1 %copy-start.1 = (bf16[32,16,2048]{2,1,0:T(8,128)(2,1)}, bf16[32,16,2048]{2,1,0:T(8,128)(2,1)S(1)}, u32[]{:S(2)}) copy-start(bf16[32,16,2048]{2,1,0:T(8,128)(2,1)S(1)} %all_to_all.10) | copy-start | bytes 6291460
  50.1 7.4 %copy-start.8 = (s32[128]{0:T(128)S(1)}, s32[128]{0:T(128)}, u32[]{:S(2)}) copy-start(s32[128]{0:T(128)} %param.29) | copy-start | bytes 1540
  50.2 7.5 %copy-start.6 = (bf16[128,64]{0,1:T(8,128)(2,1)S(1)}, bf16[128,64]{0,1:T(8,128)(2,1)}, u32[]{:S(2)}) copy-start(bf16[128,64]{0,1:T(8,128)(2,1)} %param.27) | copy-start | bytes 49156
  50.2 7.7 %copy-start.5 = (s32[128,64]{0,1:T(8,128)S(1)}, s32[128,64]{0,1:T(8,128)}, u32[]{:S(2)}) copy-start(s32[128,64]{0,1:T(8,128)} %param.26) | copy-start | bytes 98308
  50.2 7.8 %copy-start.2 = (bf16[128,64,64]{0,2,1:T(8,128)(2,1)S(1)}, bf16[128,64,64]{0,2,1:T(8,128)(2,1)}, u32[]{:S(2)}) copy-start(bf16[128,64,64]{0,2,1:T(8,128)(2,1)} %param.28) | copy-start | bytes 3145732
  50.2 32.8 %all-to-all-start = ((bf16[32,16,2048]{2,1,0:T(8,128)(2,1)}), bf16[32,16,2048]{2,1,0:T(8,128)(2,1)}, u32[]{:S(2)}, u32[]{:S(2)}) async-start(bf16[32,16,2048]{2,1,0:T(8,128)(2,1)} %stack.10), calls=%async_computation | async-start | bytes 4194304 | tf_op jit(solution)/shard_map/all_to_all | solution.py:67
  57.5 292.0 %all-reduce.6.cloned.1.call-start = ((), (), s32[]{:S(2)}) async-start(), calls=%async_computation.2 | async-start | bytes 2097152 | tf_op jit(solution)/shard_map/psum | solution.py:83
  173.9 52.6 %copy-start.7 = (s32[128]{0:T(128)S(1)}, s32[128]{0:T(128)}, u32[]{:S(2)}) copy-start(s32[128]{0:T(128)} %param.30) | copy-start | bytes 1540
Sparse Core Ops, SparseCore 0:
  230.0 119.5 all-reduce.5
